TPU v7x, 128 devices: a whole 4x4x4 slice. The times are simulated.
128 devices in a mesh: leaf: 4 (over y), row: 8 (over z, core), col: 4 (over x).
Axes of the slice: x: 4, y: 4, z: 4, core: 2. Of those that a mesh axis runs over, the one named last changes fastest.
Arguments:
- sigma_top: float32 [1024, 1024], P(('leaf', 'row'), 'col')
- panels: float32 [4, 7, 1024, 512], P('leaf', None, 'row', 'col'), may hold values from -0.1875 to 0.1875
- inverse_diag: float32 [4, 7, 512, 512], P('leaf', None, 'col')
- slot_lists: int32 [4, 6, 8], P('leaf'), may hold values from -1 to 11, as said below
- parent_links: int32 [4, 4], P('leaf'), may hold values from 1 to 2
Outputs:
- ancestor_block: float32 [4, 7, 1024, 512], P('leaf', None, 'row', 'col')
- diagonal_block: float32 [4, 7, 512, 512], P('leaf', None, None, 'col')
Inputs may be any that keep to these rules, and one draw needn't show every extreme that they name: `slot_lists`: in every row, entries 0 to 3 are 8 to 11 in order (the parent's own tiles); then come 1 to 3 distinct parent ancestor slots, below 8 for supernodes 1 and 2 and below 4 for supernodes 3 to 6; the rest are -1, so every row has padding. `parent_links`: each supernode 3 to 6 has supernode 1 or 2 as its parent. `sigma_top`: symmetric.
All inputs are finite; a program needn't handle non-finite values.
Results may differ from a plain program's by a relative error of at most 0.0001.
Values sent between devices are 32-bit elements; how exact they have to be, the bound alone decides.
A program may use at most 128 MiB of HBM per device.

v0:
```python
import jax
import jax.numpy as jnp
from jax import lax
from jax.sharding import PartitionSpec as P

TILE = 128
HIGHEST = lax.Precision.HIGHEST


def mm(a, b):
    return jnp.matmul(a, b, precision=HIGHEST, preferred_element_type=jnp.float32)


def tile_rows(matrix, index, tile):
    return lax.dynamic_slice_in_dim(matrix, index * tile, tile, 0)


def tile_cols(matrix, index, tile):
    return lax.dynamic_slice_in_dim(matrix, index * tile, tile, 1)


def scatter_factor(factor_col, slots, positions, tile):
    tiles = factor_col.reshape(slots.shape[0], tile, factor_col.shape[1])
    hits = slots[:, None] == jnp.arange(positions, dtype=slots.dtype)[None, :]
    present = jnp.any(hits, axis=0)
    source = jnp.argmax(hits, axis=0)
    moved = jnp.take(tiles, source, axis=0)
    moved = jnp.where(present[:, None, None], moved, 0.0)
    return moved.reshape(positions * tile, factor_col.shape[1])


def pick_transposed(column_block, picks, tile):
    tiles = column_block.reshape(-1, tile, tile)
    chosen = jnp.take(tiles, jnp.maximum(picks, 0), axis=0)
    chosen = jnp.where((picks >= 0)[:, None, None], chosen, 0.0)
    return jnp.transpose(chosen, (2, 0, 1)).reshape(tile, picks.shape[0] * tile)


def body(sigma_top, panels, inverse_diag, slot_lists, parent_links):
    tile = TILE
    row_count = lax.axis_size("row")
    col_count = lax.axis_size("col")
    leaf_count = lax.axis_size("leaf")
    r = lax.axis_index("row")
    c = lax.axis_index("col")
    panel = panels[0]
    inverse = inverse_diag[0]
    picks_all = slot_lists[0]
    parents = parent_links[0]
    nodes = panel.shape[0]
    width = inverse.shape[2]
    own_tiles = width // tile
    slot_count = picks_all.shape[1]
    positions = slot_count + own_tiles
    band = width // row_count
    partial_factor = mm(panel, inverse)
    factor_rows = lax.psum(partial_factor, "col")
    living = jnp.concatenate([jnp.ones((1, slot_count), jnp.bool_), picks_all >= 0], axis=0)
    live_here = jnp.take(living, r, axis=1).astype(jnp.float32)
    factor_rows = factor_rows * live_here[:, None, None]
    factor_tile = lax.dynamic_slice_in_dim(factor_rows, c * tile, tile, 2)
    factor_cols = lax.all_gather(factor_tile, "row", axis=1, tiled=True)
    inverse_band = lax.dynamic_slice_in_dim(inverse, r * band, band, 2)
    partial_gram = mm(jnp.transpose(inverse_band, (0, 2, 1)), inverse)
    gram_piece = lax.psum_scatter(partial_gram, "col", scatter_dimension=2, tiled=True)
    local_rows, local_cols = sigma_top.shape
    gathered = lax.all_gather(sigma_top, ("leaf", "row", "col"), axis=0)
    sigma = gathered.reshape(leaf_count * row_count, col_count, local_rows, local_cols)
    sigma = jnp.transpose(sigma, (0, 2, 1, 3)).reshape(
        leaf_count * row_count * local_rows, col_count * local_cols
    )

    def diag_partial(first, products):
        rows = factor_rows[first : first + products.shape[0]]
        return mm(jnp.transpose(rows, (0, 2, 1)), products)

    def reduce_and_gather(first, products):
        count = products.shape[0]
        piece = lax.psum_scatter(
            diag_partial(first, products), "row", scatter_dimension=1, tiled=True
        )
        piece = piece + gram_piece[first : first + count]
        both = jnp.concatenate([products, piece], axis=1)
        everything = lax.all_gather(both, ("row", "col"), axis=0)
        everything = everything.reshape(row_count, col_count, count, tile + band, tile)
        product_full = jnp.transpose(everything[:, :, :, :tile], (2, 0, 3, 1, 4)).reshape(
            count, row_count * tile, col_count * tile
        )
        diag_full = jnp.transpose(everything[:, :, :, tile:], (2, 0, 3, 1, 4)).reshape(
            count, row_count * band, col_count * tile
        )
        return (product_full, diag_full)

    own_row = jnp.minimum(r, own_tiles - 1)
    upper = r < own_tiles
    product_0 = mm(tile_rows(sigma, r, tile), factor_cols[0])
    product_full_0, diag_full_0 = reduce_and_gather(0, product_0[None])
    product_full_0 = product_full_0[0]
    diag_full_0 = diag_full_0[0]
    level_1 = []
    for node in (1, 2):
        slots = picks_all[node - 1]
        spread = scatter_factor(factor_cols[node], slots, positions, tile)
        top_row = jnp.concatenate(
            [
                -jnp.transpose(tile_cols(product_full_0, own_row, tile)),
                tile_rows(diag_full_0, own_row, tile),
            ],
            axis=1,
        )
        source = slots[jnp.maximum(r, own_tiles)]
        source_row = jnp.maximum(source, 0)
        low_row = jnp.concatenate(
            [tile_rows(sigma, source_row, tile), -tile_rows(product_full_0, source_row, tile)],
            axis=1,
        )
        low_row = jnp.where(source >= 0, low_row, 0.0)
        row = jnp.where(upper, top_row, low_row)
        level_1.append(mm(row, spread))
    product_1 = jnp.stack(level_1)
    product_full_1, diag_full_1 = reduce_and_gather(1, product_1)
    level_2 = []
    for node in range(3, nodes):
        slots = picks_all[node - 1]
        parent = parents[node - 3] - 1
        parent_slots = jnp.take(picks_all, parent, axis=0)
        product_p = jnp.take(product_full_1, parent, axis=0)
        diag_p = jnp.take(diag_full_1, parent, axis=0)
        spread = scatter_factor(factor_cols[node], slots, positions, tile)
        top_row = jnp.concatenate(
            [-jnp.transpose(tile_cols(product_p, own_row, tile)), tile_rows(diag_p, own_row, tile)],
            axis=1,
        )
        source = slots[jnp.maximum(r, own_tiles)]
        source_row = jnp.clip(source, 0, own_tiles - 1)
        corner = pick_transposed(
            -tile_cols(product_full_0, source_row, tile), parent_slots[own_tiles:], tile
        )
        low_row = jnp.concatenate(
            [
                tile_rows(diag_full_0, source_row, tile),
                corner,
                -tile_rows(product_p, source_row, tile),
            ],
            axis=1,
        )
        low_row = jnp.where(source >= 0, low_row, 0.0)
        row = jnp.where(upper, top_row, low_row)
        level_2.append(mm(row, spread))
    product_2 = jnp.stack(level_2)
    first_2 = 3
    count_2 = product_2.shape[0]
    gram_rows = jnp.zeros((count_2, width, tile), jnp.float32)
    gram_rows = lax.dynamic_update_slice_in_dim(
        gram_rows, gram_piece[first_2 : first_2 + count_2], r * band, 1
    )
    diag_2 = lax.psum(diag_partial(first_2, product_2) + gram_rows, "row")
    products = jnp.concatenate([product_0[None], product_1, product_2], axis=0)
    diag_cols = jnp.concatenate(
        [
            tile_cols(diag_full_0, c, tile)[None],
            lax.dynamic_slice_in_dim(diag_full_1, c * tile, tile, 2),
            diag_2,
        ],
        axis=0,
    )
    return ((-products)[None], diag_cols[None])


def solution(mesh):
    return jax.shard_map(
        body,
        mesh=mesh,
        in_specs=(
            P(("leaf", "row"), "col"),
            P("leaf", None, "row", "col"),
            P("leaf", None, "col", None),
            P("leaf", None, None),
            P("leaf", None),
        ),
        out_specs=(P("leaf", None, "row", "col"), P("leaf", None, None, "col")),
        check_vma=False,
    )
```

profile of v0, /device:TPU:0, one launch (start us, length us, event | category | flops | bytes accessed | tf_op | source)
XLA Modules:
  0.0 459.2 jit_solution(14943117877159287603)
XLA Ops:
  9.5 3.9 fusion.2
  14.3 57.6 %all-reduce.4.cloned.1.call-done = f32[7,128,512]{2,1,0:T(8,128)} async-done(((f32[7,128,512]{2,1,0:T(8,128)}), f32[7,128,512]{2,1,0:T(8,128)}) %all-reduce.4.cloned.1.call-update) | async-done | bytes 1835024 | tf_op jit(solution)/shard_map/psum | solution.py:57
  75.9 2.3 fusion
  78.3 18.1 %all-gather.10.cloned.1.call-done = f32[4096,256]{1,0:T(8,128)} async-done(((f32[32,256]{1,0:T(8,128)}), f32[4096,256]{1,0:T(8,128)}) %all-gather.10.cloned.1.call-update) | async-done | bytes 4194320 | tf_op jit(solution)/shard_map/all_gather | solution.py:67
  96.3 5.8 %copy.83 = f32[32,4,32,256]{3,1,2,0:T(4,128)S(1)} copy(f32[32,4,32,256]{3,2,1,0:T(8,128)} %bitcast.194) | data formatting | bytes 8388608 | tf_op jit(solution)/shard_map/reshape | solution.py:68
  102.2 3.0 copy.124
  105.1 20.2 %all-gather.8.cloned.1.call-done = f32[7,1024,128]{2,1,0:T(8,128)} async-done(((f32[7,128,128]{2,1,0:T(8,128)}), f32[7,1024,128]{2,1,0:T(8,128)}) %all-gather.8.cloned.1.call-update) | async-done | bytes 3670032 | tf_op jit(solution)/shard_map/all_gather | solution.py:62
  125.3 2.5 bitcast_dynamic-update-slice_fusion.6
  129.2 30.5 %reduce-scatter.4.cloned.1.call-done = f32[1,64,128]{2,1,0:T(8,128)} async-done(((f32[1,512,128]{2,1,0:T(8,128)}), f32[1,64,128]{2,1,0:T(8,128)}) %reduce-scatter.4.cloned.1.call-update) | async-done | bytes 32784 | tf_op jit(solution)/shard_map/reduce_scatter | solution.py:79
  170.4 3.1 fusion.102
  182.0 23.9 %all-gather.12.cloned.1.call-done = f32[32,192,128]{2,1,0:T(8,128)} async-done(((f32[1,192,128]{2,1,0:T(8,128)}), f32[32,192,128]{2,1,0:T(8,128)}) %all-gather.12.cloned.1.call-update) | async-done | bytes 3145744 | tf_op jit(solution)/shard_map/all_gather | solution.py:84
  207.3 3.2 slice.189
  210.5 2.9 copy.114
  224.9 2.9 bitcast_dynamic-update-slice_fusion.5
  231.2 30.5 %reduce-scatter.8.cloned.1.call-done = f32[2,64,128]{2,1,0:T(8,128)} async-done(((f32[2,512,128]{2,1,0:T(8,128)}), f32[2,64,128]{2,1,0:T(8,128)}) %reduce-scatter.8.cloned.1.call-update) | async-done | bytes 65552 | tf_op jit(solution)/shard_map/reduce_scatter | solution.py:79
  274.2 2.5 gather_fusion.7
  280.4 2.3 select_select_fusion.1
  299.2 12.6 %all-gather.14.cloned.1.call-done = f32[64,192,128]{2,1,0:T(8,128)} async-done(((f32[2,192,128]{2,1,0:T(8,128)}), f32[64,192,128]{2,1,0:T(8,128)}) %all-gather.14.cloned.1.call-update) | async-done | bytes 6291472 | tf_op jit(solution)/shard_map/all_gather | solution.py:84
  311.9 3.2 slice.195
  315.0 4.7 %slice.194 = f32[8,4,2,128,128]{4,3,2,1,0:T(8,128)} slice(f32[8,4,2,192,128]{4,3,2,1,0:T(8,128)} %bitcast.193), slice={[0:8], [0:4], [0:2], [0:128], [0:128]} | slice | bytes 8388608 | tf_op jit(solution)/shard_map/slice | solution.py:86
  319.8 5.3 %copy.118 = f32[8,4,2,128,128]{3,0,4,1,2:T(8,128)} copy(f32[8,4,2,128,128]{4,3,2,1,0:T(8,128)} %slice.194) | data formatting | bytes 8388608
  325.0 4.9 %reshape.293 = f32[2,1024,512]{1,2,0:T(8,128)} reshape(f32[2,8,128,4,128]{2,1,4,3,0:T(8,128)} %bitcast.183) | data formatting | bytes 8388608 | tf_op jit(solution)/shard_map/reshape | solution.py:86
  329.9 4.3 copy.134
  334.2 3.1 reshape.294
  337.3 4.2 select_bitcast_fusion.4
  345.8 7.9 %select_bitcast_fusion = (f32[1024,512]{0,1:T(8,128)}, f32[1,1024,512]{1,2,0:T(8,128)}, f32[1,1024,512]{1,2,0:T(8,128)}, f32[1,1024,512]{1,2,0:T(8,128)}) fusion(f32[2,1024,512]{1,2,0:T(8,128)} %reshape.293, s32[]{:T(128)S(6)} %select_n.346, pred[]{:T(512)S(6)} %and.78, s32[]{:T(128)S(6)} %select_n.326, s32[]{:T(128)S(6)} %select_n.316, s32[]{:T(128)S(6)} %select_n.336), kind=kLoop, calls=%fused_computation.12 | loop fusion | flops 524288 | bytes 16777232 | tf_op jit(solution)/shard_map/jit(_take)/select_n | solution.py:127
  353.6 2.9 copy.121
  363.7 3.0 copy.119
  370.6 2.9 copy.122
  377.5 3.3 bitcast_dynamic-update-slice_fusion.3
  391.4 57.6 %all-reduce.6.cloned.1.call-done = f32[4,512,128]{2,1,0:T(8,128)} async-done(((f32[4,512,128]{2,1,0:T(8,128)}), f32[4,512,128]{2,1,0:T(8,128)}) %all-reduce.6.cloned.1.call-update) | async-done | bytes 1048592 | tf_op jit(solution)/shard_map/psum | solution.py:157
  449.1 2.6 maximum_bitcast_fusion
  (217 shorter events, 95.1 us)
Async XLA Ops:
  8.0 6.0 %copy-start.37 = (s32[1,6,8]{2,0,1:T(1,128)S(1)}, s32[1,6,8]{2,0,1:T(1,128)}, u32[]{:S(2)}) copy-start(s32[1,6,8]{2,0,1:T(1,128)} %param.18) | copy-start | bytes 580
  8.0 63.9 %all-reduce.4.cloned.1.call-start = ((), (), s32[]{:S(2)}) async-start(), calls=%async_computation.3 | async-start | bytes 3670016 | tf_op jit(solution)/shard_map/psum | solution.py:57
  13.4 82.9 %all-gather.10.cloned.1.call-start = ((), (), s32[]{:S(2)}) async-start(), calls=%async_computation.9 | async-start | bytes 4227072 | tf_op jit(solution)/shard_map/all_gather | solution.py:67
  14.0 111.3 %all-gather.8.cloned.1.call-start = ((), (), s32[]{:S(2)}) async-start(), calls=%async_computation.4 | async-start | bytes 4128768 | tf_op jit(solution)/shard_map/all_gather | solution.py:62
  75.8 53.4 %reduce-scatter.6.cloned.1.call-start = ((), (), s32[]{:S(2)}) async-start(), calls=%async_computation.6 | async-start | bytes 1146880 | tf_op jit(solution)/shard_map/reduce_scatter | solution.py:65
  78.2 81.5 %reduce-scatter.4.cloned.1.call-start = ((), (), s32[]{:S(2)}) async-start(), calls=%async_computation.5 | async-start | bytes 294912 | tf_op jit(solution)/shard_map/reduce_scatter | solution.py:79
  102.1 25.6 %copy-start.3 = (f32[7,128,512]{2,1,0:T(8,128)S(1)}, f32[7,128,512]{2,1,0:T(8,128)}, u32[]{:S(2)}) copy-start(f32[7,128,512]{2,1,0:T(8,128)} %copy-done.2) | copy-start | bytes 5505028
  129.1 76.9 %all-gather.12.cloned.1.call-start = ((), (), s32[]{:S(2)}) async-start(), calls=%async_computation.10 | async-start | bytes 3244032 | tf_op jit(solution)/shard_map/all_gather | solution.py:84
  161.2 100.5 %reduce-scatter.8.cloned.1.call-start = ((), (), s32[]{:S(2)}) async-start(), calls=%async_computation.7 | async-start | bytes 589824 | tf_op jit(solution)/shard_map/reduce_scatter | solution.py:79
  223.8 4.0 copy-start.16
  223.8 4.0 copy-start.21
  223.8 4.0 copy-start.30
  229.4 34.2 %copy-start.38 = (s32[1,4]{1,0:T(1,128)S(1)}, s32[1,4]{1,0:T(1,128)}, u32[]{:S(2)}) copy-start(s32[1,4]{1,0:T(1,128)} %param.19) | copy-start | bytes 52
  229.4 47.4 %copy-start.7 = (f32[1,1024,128]{2,1,0:T(8,128)S(1)}, f32[1,1024,128]{2,1,0:T(8,128)}, u32[]{:S(2)}) copy-start(f32[1,1024,128]{2,1,0:T(8,128)} %get-tuple-element.69) | copy-start | bytes 1572868
  231.2 47.1 %copy-start.6 = (f32[1,1024,128]{2,1,0:T(8,128)S(1)}, f32[1,1024,128]{2,1,0:T(8,128)}, u32[]{:S(2)}) copy-start(f32[1,1024,128]{2,1,0:T(8,128)} %get-tuple-element.71) | copy-start | bytes 1572868
  231.2 80.7 %all-gather.14.cloned.1.call-start = ((), (), s32[]{:S(2)}) async-start(), calls=%async_computation.11 | async-start | bytes 6488064 | tf_op jit(solution)/shard_map/all_gather | solution.py:84
  263.3 185.8 %all-reduce.6.cloned.1.call-start = ((), (), s32[]{:S(2)}) async-start(), calls=%async_computation.8 | async-start | bytes 2097152 | tf_op jit(solution)/shard_map/psum | solution.py:157
  280.4 3.4 copy-start.10
  283.8 6.0 %copy-start.19 = (f32[1024,128]{0,1:T(8,128)S(1)}, f32[1024,128]{0,1:T(8,128)}, u32[]{:S(2)}) copy-start(f32[1024,128]{0,1:T(8,128)} %get-tuple-element.76) | copy-start | bytes 1572868
  285.9 7.6 %copy-start.18 = (f32[1024,128]{0,1:T(8,128)S(1)}, f32[1024,128]{0,1:T(8,128)}, u32[]{:S(2)}) copy-start(f32[1024,128]{0,1:T(8,128)} %get-tuple-element.77) | copy-start | bytes 1572868
  290.8 6.0 %copy-start.17 = (f32[1024,128]{0,1:T(8,128)S(1)}, f32[1024,128]{0,1:T(8,128)}, u32[]{:S(2)}) copy-start(f32[1024,128]{0,1:T(8,128)} %get-tuple-element.78) | copy-start | bytes 1572868
  293.7 4.9 %copy-start.22 = (f32[1024,128]{1,0:T(8,128)S(1)}, f32[1024,128]{1,0:T(8,128)}, u32[]{:S(2)}) copy-start(f32[1024,128]{1,0:T(8,128)} %copy.108) | copy-start | bytes 1572868
  359.3 4.1 copy-start.31
  377.4 3.4 copy-start.24
  377.4 3.4 copy-start.26
  377.4 3.4 copy-start.29
  377.4 5.0 %copy-start.9 = (f32[128,1536]{1,0:T(8,128)S(1)}, f32[128,1536]{1,0:T(8,128)}, u32[]{:S(2)}) copy-start(f32[128,1536]{1,0:T(8,128)} %copy.106) | copy-start | bytes 2359300
  377.4 5.0 %copy-start.14 = (f32[12,128,128]{2,1,0:T(8,128)S(1)}, f32[12,128,128]{2,1,0:T(8,128)}, u32[]{:S(2)}) copy-start(f32[12,128,128]{2,1,0:T(8,128)} %select_select_fusion.1) | copy-start | bytes 2359300
  377.4 5.0 %copy-start.23 = (f32[128,512]{1,0:T(8,128)S(1)}, f32[128,512]{1,0:T(8,128)}, u32[]{:S(2)}) copy-start(f32[128,512]{1,0:T(8,128)} %get-tuple-element.87) | copy-start | bytes 786436
  377.4 5.0 %copy-start.27 = (f32[128,512]{1,0:T(8,128)S(1)}, f32[128,512]{1,0:T(8,128)}, u32[]{:S(2)}) copy-start(f32[128,512]{1,0:T(8,128)} %dynamic-slice_negate_fusion.5) | copy-start | bytes 786436
  377.4 5.0 %copy-start.28 = (f32[128,512]{1,0:T(8,128)S(1)}, f32[128,512]{1,0:T(8,128)}, u32[]{:S(2)}) copy-start(f32[128,512]{1,0:T(8,128)} %copy.105) | copy-start | bytes 786436
  390.2 61.4 %copy-start.1 = (f32[1,7,128,512]{3,2,1,0:T(8,128)S(1)}, f32[1,7,128,512]{3,2,1,0:T(8,128)}, u32[]{:S(2)}) copy-start(f32[1,7,128,512]{3,2,1,0:T(8,128)} %param.17) | copy-start | bytes 5505028
  (16 other events, 38.9 us)
Sparse Core Ops, SparseCore 0:
  13.5 58.3 all-reduce.3
  79.1 22.6 reduce-scatter.5
  129.2 30.4 reduce-scatter.3
  162.1 43.8 all-gather.11
  231.3 30.3 reduce-scatter.7
  263.8 48.0 all-gather.13
Sparse Core Ops, SparseCore 1:
  17.0 79.3 all-gather.9
  98.5 26.8 all-gather.7
  388.5 60.5 all-reduce.5
where the time goes:
time: 461 us; the launch traced here: 459 us
  waiting for transfers between devices  252 us (55%)
  local copies, waits for them, and re-layouts  100 us (22%)
  other arithmetic  53.9 us (12%)
  between operations  26.5 us (6%)
  matrix products  26 us (6%)
    reduce_scatter x2, waiting for transfers between devices, reduce_and_gather(): lax.psum_scatter(diag_partial(first, products), 'row', scatter_dimension=...  61 us
    psum x1, waiting for transfers between devices, body(): factor_rows = lax.psum(partial_factor, 'col')  57.6 us
    psum x1, waiting for transfers between devices, body(): diag_2 = lax.psum(diag_partial(first_2, product_2) + gram_rows, 'row')  57.6 us
    all_gather x2, waiting for transfers between devices, reduce_and_gather(): everything = lax.all_gather(both, ('row', 'col'), axis=0)  36.5 us
    unnamed x92, local copies, waits for them, and re-layouts  35.4 us
    dot_general x12, matrix products, mm(): jnp.matmul(a, b, precision=HIGHEST, preferred_element_type=jnp.float32)  26 us
    all_gather x1, waiting for transfers between devices, body(): factor_cols = lax.all_gather(factor_tile, 'row', axis=1, tiled=True)  20.2 us
    all_gather x1, waiting for transfers between devices, body(): gathered = lax.all_gather(sigma_top, ('leaf', 'row', 'col'), axis=0)  18.1 us
  transfers between devices with their start and end apart: 9, of which 8 were waited for; matrix products, arithmetic and copies ran while one was open for 15% of the time, Pallas kernels for 0%

commit v1 on v0

--- a/solution.py
+++ b/solution.py
@@ -54,7 +54,11 @@
     positions = slot_count + own_tiles
     band = width // row_count
     partial_factor = mm(panel, inverse)
-    factor_rows = lax.psum(partial_factor, "col")
+    factor_rows = partial_factor
+    for hop in (1, 2):
+        factor_rows = factor_rows + lax.ppermute(
+            factor_rows, "col", [(dev, dev ^ hop) for dev in range(4)]
+        )
     living = jnp.concatenate([jnp.ones((1, slot_count), jnp.bool_), picks_all >= 0], axis=0)
     live_here = jnp.take(living, r, axis=1).astype(jnp.float32)
     factor_rows = factor_rows * live_here[:, None, None]

time: 461 us -> 479 us (1.039)
  waiting for transfers between devices: 252 us -> 264 us
  starting transfers between devices: 0.77 us -> 5.7 us
    ppermute x0 -> x2, waiting for transfers between devices: none -> 86.2 us  [body(): lax.ppermute(factor_rows, 'col', [(dev, dev ^ hop) for dev in range(4)])]
    psum x1 -> x0, waiting for transfers between devices: 57.6 us -> none  [body(): factor_rows = lax.psum(partial_factor, 'col')]
    all_gather x1, waiting for transfers between devices: 18.1 us -> 0.02 us  [body(): gathered = lax.all_gather(sigma_top, ('leaf', 'row', 'col'), axis=0)]
    ppermute x0 -> x2, starting transfers between devices: none -> 4.96 us  [body(): lax.ppermute(factor_rows, 'col', [(dev, dev ^ hop) for dev in range(4)])]
  transfers between devices with their start and end apart: 9 -> 10, of which waited for: 8 -> 8; matrix products, arithmetic and copies ran while one was open for 15% -> 15% of each run, Pallas kernels for 0% -> 0%
where the time goes in v1:
time: 479 us; the launch traced here: 477 us
  waiting for transfers between devices  264 us (55%)
  local copies, waits for them, and re-layouts  99.6 us (21%)
  other arithmetic  56.3 us (12%)
  between operations  26.2 us (5%)
  matrix products  24.8 us (5%)
  starting transfers between devices  5.7 us (1%)
    ppermute x2, waiting for transfers between devices, body(): lax.ppermute(factor_rows, 'col', [(dev, dev ^ hop) for dev in range(4)])  86.2 us
    reduce_scatter x2, waiting for transfers between devices, reduce_and_gather(): lax.psum_scatter(diag_partial(first, products), 'row', scatter_dimension=...  60.7 us
    psum x1, waiting for transfers between devices, body(): diag_2 = lax.psum(diag_partial(first_2, product_2) + gram_rows, 'row')  57.8 us
    all_gather x2, waiting for transfers between devices, reduce_and_gather(): everything = lax.all_gather(both, ('row', 'col'), axis=0)  36.8 us
    unnamed x92, local copies, waits for them, and re-layouts  34.7 us
    dot_general x12, matrix products, mm(): jnp.matmul(a, b, precision=HIGHEST, preferred_element_type=jnp.float32)  24.8 us
    all_gather x1, waiting for transfers between devices, body(): factor_cols = lax.all_gather(factor_tile, 'row', axis=1, tiled=True)  22.1 us
    select_n x4, other arithmetic, body(): product_p = jnp.take(product_full_1, parent, axis=0)  13.4 us
  transfers between devices with their start and end apart: 10, of which 8 were waited for; matrix products, arithmetic and copies ran while one was open for 15% of the time, Pallas kernels for 0%

profile of v1, /device:TPU:0, one launch (start us, length us, event | category | flops | bytes accessed | tf_op | source)
XLA Modules:
  0.0 477.0 jit_solution(6994309933131596920)
XLA Ops:
  9.5 2.6 fusion.2
  13.8 41.4 %collective-permute-done = f32[7,128,512]{2,1,0:T(8,128)S(1)} collective-permute-done((f32[7,128,512]{2,1,0:T(8,128)S(1)}, f32[7,128,512]{2,1,0:T(8,128)S(1)}, u32[]{:S(2)}, u32[]{:S(2)}) %collective-permute-start) | collective-permute-done | bytes 1835040 | tf_op jit(solution)/shard_map/ppermute | solution.py:59
  56.9 3.3 collective-permute-start.1
  60.5 44.7 %collective-permute-done.1 = f32[7,128,512]{2,1,0:T(8,128)} collective-permute-done((f32[7,128,512]{2,1,0:T(8,128)}, f32[7,128,512]{2,1,0:T(8,128)}, u32[]{:S(2)}, u32[]{:S(2)}) %collective-permute-start.1) | collective-permute-done | bytes 1835040 | tf_op jit(solution)/shard_map/ppermute | solution.py:59
  105.2 2.6 add_multiply_fusion
  112.4 5.8 %copy.83 = f32[32,4,32,256]{3,1,2,0:T(4,128)S(1)} copy(f32[32,4,32,256]{3,2,1,0:T(8,128)} %bitcast.194) | data formatting | bytes 8388608 | tf_op jit(solution)/shard_map/reshape | solution.py:72
  118.2 3.0 copy.124
  121.1 22.1 %all-gather.8.cloned.1.call-done = f32[7,1024,128]{2,1,0:T(8,128)} async-done(((f32[7,128,128]{2,1,0:T(8,128)}), f32[7,1024,128]{2,1,0:T(8,128)}) %all-gather.8.cloned.1.call-update) | async-done | bytes 3670032 | tf_op jit(solution)/shard_map/all_gather | solution.py:66
  143.2 2.5 bitcast_dynamic-update-slice_fusion.6
  147.1 30.4 %reduce-scatter.4.cloned.1.call-done = f32[1,64,128]{2,1,0:T(8,128)} async-done(((f32[1,512,128]{2,1,0:T(8,128)}), f32[1,64,128]{2,1,0:T(8,128)}) %reduce-scatter.4.cloned.1.call-update) | async-done | bytes 32784 | tf_op jit(solution)/shard_map/reduce_scatter | solution.py:83
  190.5 3.1 fusion.102
  199.8 24.1 %all-gather.12.cloned.1.call-done = f32[32,192,128]{2,1,0:T(8,128)} async-done(((f32[1,192,128]{2,1,0:T(8,128)}), f32[32,192,128]{2,1,0:T(8,128)}) %all-gather.12.cloned.1.call-update) | async-done | bytes 3145744 | tf_op jit(solution)/shard_map/all_gather | solution.py:88
  225.2 3.2 slice.189
  228.3 2.9 copy.114
  242.8 2.9 bitcast_dynamic-update-slice_fusion.5
  249.1 30.3 %reduce-scatter.8.cloned.1.call-done = f32[2,64,128]{2,1,0:T(8,128)} async-done(((f32[2,512,128]{2,1,0:T(8,128)}), f32[2,64,128]{2,1,0:T(8,128)}) %reduce-scatter.8.cloned.1.call-update) | async-done | bytes 65552 | tf_op jit(solution)/shard_map/reduce_scatter | solution.py:83
  292.0 2.5 gather_fusion.7
  317.0 12.7 %all-gather.14.cloned.1.call-done = f32[64,192,128]{2,1,0:T(8,128)} async-done(((f32[2,192,128]{2,1,0:T(8,128)}), f32[64,192,128]{2,1,0:T(8,128)}) %all-gather.14.cloned.1.call-update) | async-done | bytes 6291472 | tf_op jit(solution)/shard_map/all_gather | solution.py:88
  329.7 3.2 slice.195
  332.9 4.7 slice.194
  337.6 5.3 %copy.118 = f32[8,4,2,128,128]{3,0,4,1,2:T(8,128)} copy(f32[8,4,2,128,128]{4,3,2,1,0:T(8,128)} %slice.194) | data formatting | bytes 8388608
  342.9 4.9 %reshape.293 = f32[2,1024,512]{1,2,0:T(8,128)} reshape(f32[2,8,128,4,128]{2,1,4,3,0:T(8,128)} %bitcast.183) | data formatting | bytes 8388608 | tf_op jit(solution)/shard_map/reshape | solution.py:90
  347.7 4.3 copy.134
  352.1 3.1 reshape.294
  355.2 4.2 select_bitcast_fusion.4
  363.6 7.9 %select_bitcast_fusion = (f32[1024,512]{0,1:T(8,128)}, f32[1,1024,512]{1,2,0:T(8,128)}, f32[1,1024,512]{1,2,0:T(8,128)}, f32[1,1024,512]{1,2,0:T(8,128)}) fusion(f32[2,1024,512]{1,2,0:T(8,128)} %reshape.293, s32[]{:T(128)S(6)} %select_n.346, pred[]{:T(512)S(6)} %and.78, s32[]{:T(128)S(6)} %select_n.326, s32[]{:T(128)S(6)} %select_n.316, s32[]{:T(128)S(6)} %select_n.336), kind=kLoop, calls=%fused_computation.12 | loop fusion | flops 524288 | bytes 16777232 | tf_op jit(solution)/shard_map/jit(_take)/select_n | solution.py:131
  371.5 2.9 copy.121
  381.6 3.0 copy.119
  388.4 2.9 copy.122
  395.3 3.3 bitcast_dynamic-update-slice_fusion.3
  409.3 57.8 %all-reduce.3.cloned.1.call-done = f32[4,512,128]{2,1,0:T(8,128)} async-done(((f32[4,512,128]{2,1,0:T(8,128)}), f32[4,512,128]{2,1,0:T(8,128)}) %all-reduce.3.cloned.1.call-update) | async-done | bytes 1048592 | tf_op jit(solution)/shard_map/psum | solution.py:161
  467.1 2.6 maximum_bitcast_fusion
  (219 shorter events, 100.7 us)
Async XLA Ops:
  8.0 104.3 %all-gather.10.cloned.1.call-start = ((), (), s32[]{:S(2)}) async-start(), calls=%async_computation.8 | async-start | bytes 4227072 | tf_op jit(solution)/shard_map/all_gather | solution.py:71
  8.7 134.5 %all-gather.8.cloned.1.call-start = ((), (), s32[]{:S(2)}) async-start(), calls=%async_computation.3 | async-start | bytes 4128768 | tf_op jit(solution)/shard_map/all_gather | solution.py:66
  12.2 48.1 %copy-start.37 = (s32[1,6,8]{2,0,1:T(1,128)S(1)}, s32[1,6,8]{2,0,1:T(1,128)}, u32[]{:S(2)}) copy-start(s32[1,6,8]{2,0,1:T(1,128)} %param.18) | copy-start | bytes 580
  12.2 43.1 %collective-permute-start = (f32[7,128,512]{2,1,0:T(8,128)S(1)}, f32[7,128,512]{2,1,0:T(8,128)S(1)}, u32[]{:S(2)}, u32[]{:S(2)}) collective-permute-start(f32[7,128,512]{2,1,0:T(8,128)S(1)} %fusion.2), channel_id=1, source_target_pairs={{0,1},{1,0},{2,3},{3,2},{4,5},{5,4},{6,7},{7,6},{8,9},{9,8},{10,11... | collective-permute-start | bytes 5505032 | tf_op jit(solution)/shard_map/ppermute | solution.py:59
  56.9 48.3 %collective-permute-start.1 = (f32[7,128,512]{2,1,0:T(8,128)}, f32[7,128,512]{2,1,0:T(8,128)}, u32[]{:S(2)}, u32[]{:S(2)}) collective-permute-start(f32[7,128,512]{2,1,0:T(8,128)} %add.120), channel_id=1, source_target_pairs={{0,2},{1,3},{2,0},{3,1},{4,6},{5,7},{6,4},{7,5},{8,10},{9,11},{10,... | collective-permute-start | bytes 5505032 | tf_op jit(solution)/shard_map/ppermute | solution.py:59
  109.9 37.2 %reduce-scatter.6.cloned.1.call-start = ((), (), s32[]{:S(2)}) async-start(), calls=%async_computation.5 | async-start | bytes 1146880 | tf_op jit(solution)/shard_map/reduce_scatter | solution.py:69
  112.3 65.2 %reduce-scatter.4.cloned.1.call-start = ((), (), s32[]{:S(2)}) async-start(), calls=%async_computation.4 | async-start | bytes 294912 | tf_op jit(solution)/shard_map/reduce_scatter | solution.py:83
  118.1 27.6 %copy-start.3 = (f32[7,128,512]{2,1,0:T(8,128)S(1)}, f32[7,128,512]{2,1,0:T(8,128)}, u32[]{:S(2)}) copy-start(f32[7,128,512]{2,1,0:T(8,128)} %copy-done.2) | copy-start | bytes 5505028
  147.0 76.8 %all-gather.12.cloned.1.call-start = ((), (), s32[]{:S(2)}) async-start(), calls=%async_computation.9 | async-start | bytes 3244032 | tf_op jit(solution)/shard_map/all_gather | solution.py:88
  179.0 100.5 %reduce-scatter.8.cloned.1.call-start = ((), (), s32[]{:S(2)}) async-start(), calls=%async_computation.6 | async-start | bytes 589824 | tf_op jit(solution)/shard_map/reduce_scatter | solution.py:83
  241.7 4.0 copy-start.16
  241.7 4.0 copy-start.20
  241.7 4.0 copy-start.30
  247.3 34.1 %copy-start.38 = (s32[1,4]{1,0:T(1,128)S(1)}, s32[1,4]{1,0:T(1,128)}, u32[]{:S(2)}) copy-start(s32[1,4]{1,0:T(1,128)} %param.19) | copy-start | bytes 52
  247.3 47.3 %copy-start.7 = (f32[1,1024,128]{2,1,0:T(8,128)S(1)}, f32[1,1024,128]{2,1,0:T(8,128)}, u32[]{:S(2)}) copy-start(f32[1,1024,128]{2,1,0:T(8,128)} %get-tuple-element.69) | copy-start | bytes 1572868
  249.1 47.0 %copy-start.6 = (f32[1,1024,128]{2,1,0:T(8,128)S(1)}, f32[1,1024,128]{2,1,0:T(8,128)}, u32[]{:S(2)}) copy-start(f32[1,1024,128]{2,1,0:T(8,128)} %get-tuple-element.71) | copy-start | bytes 1572868
  249.1 80.6 %all-gather.14.cloned.1.call-start = ((), (), s32[]{:S(2)}) async-start(), calls=%async_computation.10 | async-start | bytes 6488064 | tf_op jit(solution)/shard_map/all_gather | solution.py:88
  281.1 186.0 %all-reduce.3.cloned.1.call-start = ((), (), s32[]{:S(2)}) async-start(), calls=%async_computation.7 | async-start | bytes 2097152 | tf_op jit(solution)/shard_map/psum | solution.py:161
  298.2 3.4 copy-start.10
  301.6 6.0 %copy-start.19 = (f32[1024,128]{0,1:T(8,128)S(1)}, f32[1024,128]{0,1:T(8,128)}, u32[]{:S(2)}) copy-start(f32[1024,128]{0,1:T(8,128)} %get-tuple-element.76) | copy-start | bytes 1572868
  303.7 7.6 %copy-start.18 = (f32[1024,128]{0,1:T(8,128)S(1)}, f32[1024,128]{0,1:T(8,128)}, u32[]{:S(2)}) copy-start(f32[1024,128]{0,1:T(8,128)} %get-tuple-element.77) | copy-start | bytes 1572868
  308.6 6.0 %copy-start.17 = (f32[1024,128]{0,1:T(8,128)S(1)}, f32[1024,128]{0,1:T(8,128)}, u32[]{:S(2)}) copy-start(f32[1024,128]{0,1:T(8,128)} %get-tuple-element.78) | copy-start | bytes 1572868
  311.4 4.9 %copy-start.22 = (f32[1024,128]{1,0:T(8,128)S(1)}, f32[1024,128]{1,0:T(8,128)}, u32[]{:S(2)}) copy-start(f32[1024,128]{1,0:T(8,128)} %copy.108) | copy-start | bytes 1572868
  377.1 4.1 copy-start.31
  395.2 3.4 copy-start.26
  395.3 3.4 copy-start.29
  395.3 5.0 %copy-start.9 = (f32[128,1536]{1,0:T(8,128)S(1)}, f32[128,1536]{1,0:T(8,128)}, u32[]{:S(2)}) copy-start(f32[128,1536]{1,0:T(8,128)} %copy.106) | copy-start | bytes 2359300
  395.3 5.0 %copy-start.14 = (f32[12,128,128]{2,1,0:T(8,128)S(1)}, f32[12,128,128]{2,1,0:T(8,128)}, u32[]{:S(2)}) copy-start(f32[12,128,128]{2,1,0:T(8,128)} %select_select_fusion.1) | copy-start | bytes 2359300
  395.3 5.0 %copy-start.23 = (f32[128,512]{1,0:T(8,128)S(1)}, f32[128,512]{1,0:T(8,128)}, u32[]{:S(2)}) copy-start(f32[128,512]{1,0:T(8,128)} %get-tuple-element.87) | copy-start | bytes 786436
  395.3 5.0 %copy-start.27 = (f32[128,512]{1,0:T(8,128)S(1)}, f32[128,512]{1,0:T(8,128)}, u32[]{:S(2)}) copy-start(f32[128,512]{1,0:T(8,128)} %dynamic-slice_negate_fusion.5) | copy-start | bytes 786436
  395.3 5.0 %copy-start.28 = (f32[128,512]{1,0:T(8,128)S(1)}, f32[128,512]{1,0:T(8,128)}, u32[]{:S(2)}) copy-start(f32[128,512]{1,0:T(8,128)} %copy.105) | copy-start | bytes 786436
  408.1 61.6 %copy-start.1 = (f32[1,7,128,512]{3,2,1,0:T(8,128)S(1)}, f32[1,7,128,512]{3,2,1,0:T(8,128)}, u32[]{:S(2)}) copy-start(f32[1,7,128,512]{3,2,1,0:T(8,128)} %param.17) | copy-start | bytes 5505028
  (17 other events, 42.3 us)
Sparse Core Ops, SparseCore 0:
  12.0 71.4 all-gather.9
  110.0 33.1 all-gather.7
  406.4 60.6 all-reduce.2
Sparse Core Ops, SparseCore 1:
  112.8 25.9 reduce-scatter.5
  147.1 30.4 reduce-scatter.3
  179.9 43.9 all-gather.11
  249.2 30.2 reduce-scatter.7
  281.8 47.9 all-gather.13
